TPU v7x, 32 devices: a whole 2x2x4 slice. The times are simulated.
32 devices in a mesh: group: 1, req: 4 (over z), head: 4 (over y, x), pool: 2 (over core).
Axes of the slice: x: 2, y: 2, z: 4, core: 2. Of those that a mesh axis runs over, the one named last changes fastest.
Arguments:
- queries: bfloat16 [192, 4096], P(('group', 'req'), 'head'), may hold values from -128 to 128
- new_entries: bfloat16 [192, 2, 4, 256], P(('group', 'req'), None, 'head'), may hold values from -6 to 6
- cache_pages: bfloat16 [4, 416, 16, 256], P('head', ('group', 'req', 'pool')), may hold values from -6 to 6
- page_table: int32 [192, 2, 1], P(('group', 'req'), 'pool'), may hold values from 0 to 51, as said below
- cached_length: int32 [192, 2], P(('group', 'req'), 'pool'), may hold values from 1 to 16, as said below
- leave_slots: int32 [32], P(('group', 'req', 'pool')), may hold values from 0 to 50, as said below
- arrive_slots: int32 [32], P(('group', 'req', 'pool')), may hold values from 0 to 51, as said below
- residual: bfloat16 [192, 2048], P(('group', 'req', 'head')), may hold values from -5 to 5
- norm_gain: float32 [2048], replicated, may hold values from 0.5 to 1.5
- output_weight: bfloat16 [4096, 2048], P(('head', 'pool')), may hold values from -0.25 to 0.25
- expert_choice: int32 [192, 8], P(('group', 'req', 'head')), may hold values from 0 to 15, all different within a row; in each aligned block of 12 rows (0 to 11, 12 to 23, ...) at most 12 rows name the same one
- route_weight: float32 [192, 8], P(('group', 'req', 'head')), may hold values from 0.2 to 1
- gate_up: bfloat16 [16, 2, 384, 2048], P(('req', 'head'), None, 'pool'), may hold values from -0.125 to 0.125
- down_weight: bfloat16 [16, 384, 2048], P(('req', 'head'), 'pool'), may hold values from -0.3125 to 0.3125
Outputs:
- decoded: bfloat16 [192, 2048], P(('group', 'req', 'head'), 'pool')
Inputs may be any that keep to these rules, and one draw needn't show every extreme that they name: `page_table`: within each block of one index of req and one pool, the 48 entries name distinct slots, none of them among that block's leave_slots. `leave_slots`: each block's 4 entries are distinct. `arrive_slots`: each block's 4 entries are distinct slots that its page table names. `cached_length`: in every block of 48 requests and each pool some request has 16. `expert_choice`: each row names 8 distinct experts; in each aligned block of 12 rows no expert is named more than 12 times, a bound that some block reaches.
All inputs are finite; a program needn't handle non-finite values.
Results may differ from a plain program's by a relative error of at most 0.023.
Values may be sent and summed in bfloat16 or wider, within the bound.
A program may use at most 64 MiB of HBM per device.

v0:
```python
import jax
import jax.numpy as jnp
from jax import lax
from jax.sharding import PartitionSpec as P


def swapped(value, axis, apart):
    mask = 2**apart
    pairs = [(source, source ^ mask) for source in range(lax.axis_size(axis))]
    return lax.ppermute(value, axis, pairs)


def combined_all(shard, axis, join):
    gathered = jax.tree.map(
        lambda a, kind: lax.all_gather(a.astype(kind), axis),
        shard,
        (jnp.bfloat16, jnp.bfloat16, jnp.bfloat16),
    )

    def take(source):
        return jax.tree.map(
            lambda a, own: lax.dynamic_index_in_dim(a, source, 0, False).astype(own.dtype),
            gathered,
            shard,
        )

    return lax.fori_loop(
        1, lax.axis_size(axis), lambda source, state: join(state, take(source)), take(0)
    )


def merge_parts(earlier, later):
    first_max, first_denominator, first_value = earlier
    second_max, second_denominator, second_value = later
    largest = jnp.maximum(first_max, second_max)
    first_scale = jnp.exp(first_max - largest)
    second_scale = jnp.exp(second_max - largest)
    denominator = first_denominator * first_scale + second_denominator * second_scale
    weighted = first_value * first_scale[..., None] + second_value * second_scale[..., None]
    return (largest, denominator, weighted)


def local(
    queries,
    new_entries,
    cache_pages,
    page_table,
    cached_length,
    leave_slots,
    arrive_slots,
    residual,
    norm_gain,
    output_weight,
    expert_choice,
    route_weight,
    gate_up,
    down_weight,
):
    batch_size = queries.shape[0]
    group_count = cache_pages.shape[0]
    head_dim = new_entries.shape[3] // 2
    group_size = queries.shape[1] // (group_count * head_dim)
    pool_index = lax.axis_index("pool")
    outgoing = cache_pages[:, leave_slots]
    arrived = swapped(outgoing, "pool", 0)
    current = cache_pages.at[:, arrive_slots].set(arrived)
    context = current[:, page_table[:, 0, :]]
    context = context.reshape(group_count, batch_size, -1, 2 * head_dim)
    context_keys = context[..., :head_dim]
    context_values = context[..., head_dim:]
    grouped_queries = queries.reshape(batch_size, group_count, group_size, head_dim)
    score_scale = head_dim ** (-0.5)
    attention_scores = (
        jnp.einsum(
            "bgqd,gbtd->bgqt", grouped_queries, context_keys, preferred_element_type=jnp.float32
        )
        * score_scale
    )
    positions = jnp.arange(context.shape[2], dtype=jnp.int32)
    valid_mask = positions[None, :] < cached_length
    attention_scores = jnp.where(valid_mask[:, None, None, :], attention_scores, -jnp.inf)
    fresh_scores = (
        jnp.einsum(
            "bgqd,bsgd->bgqs",
            grouped_queries,
            new_entries[..., :head_dim],
            preferred_element_type=jnp.float32,
        )
        * score_scale
    )
    fresh_scores = jnp.where(pool_index == 0, fresh_scores, -jnp.inf)
    largest = jnp.maximum(jnp.max(attention_scores, axis=-1), jnp.max(fresh_scores, axis=-1))
    local_weights = jnp.exp(attention_scores - largest[..., None])
    fresh_weights = jnp.exp(fresh_scores - largest[..., None])
    denominator = jnp.sum(local_weights, axis=-1) + jnp.sum(fresh_weights, axis=-1)
    weighted = jnp.einsum("bgqt,gbtd->bgqd", local_weights, context_values.astype(jnp.float32))
    weighted = weighted + jnp.einsum(
        "bgqs,bsgd->bgqd", fresh_weights, new_entries[..., head_dim:].astype(jnp.float32)
    )
    largest, denominator, weighted = combined_all(
        (largest, denominator, weighted), "pool", merge_parts
    )
    attended = (weighted / denominator[..., None]).reshape(batch_size, -1).astype(jnp.bfloat16)
    head_width = output_weight.shape[0]
    own_heads = lax.dynamic_slice_in_dim(attended, pool_index * head_width, head_width, 1)
    partial_value = jnp.dot(own_heads, output_weight, preferred_element_type=jnp.float32)
    rows_here = residual.shape[0]
    summed = lax.psum(partial_value.astype(jnp.bfloat16), ("head", "pool")).astype(jnp.float32)
    attention = lax.dynamic_slice_in_dim(summed, lax.axis_index("head") * rows_here, rows_here, 0)
    hidden = residual.astype(jnp.float32) + attention
    normed = (
        hidden * lax.rsqrt(jnp.mean(hidden * hidden, axis=-1, keepdims=True) + 1e-06) * norm_gain
    ).astype(jnp.bfloat16)
    expert_count = lax.axis_size("req") * lax.axis_size("head")
    top_count = expert_choice.shape[1]
    capacity = max(
        2, min(rows_here, (2 * rows_here * top_count + expert_count - 1) // expert_count)
    )
    flat_choice = expert_choice.reshape(-1)
    expert_hits = (
        flat_choice[:, None] == jnp.arange(expert_count, dtype=jnp.int32)[None, :]
    ).astype(jnp.int32)
    earlier = jnp.cumsum(expert_hits, axis=0) - expert_hits
    slot_index = jnp.sum(earlier * expert_hits, axis=1)
    target = flat_choice * capacity + slot_index
    placed = (
        target[:, None] == jnp.arange(expert_count * capacity, dtype=jnp.int32)[None, :]
    ).astype(jnp.float32)
    placed = placed.reshape(rows_here, top_count, expert_count * capacity)
    dispatch = jnp.sum(placed, axis=1).astype(jnp.bfloat16)
    combine_matrix = jnp.sum(placed * route_weight[:, :, None], axis=1)
    outgoing_rows = jnp.einsum("re,rd->ed", dispatch, normed, preferred_element_type=jnp.float32)
    outgoing_rows = outgoing_rows.astype(jnp.bfloat16).reshape(expert_count, capacity, -1)
    model_width = normed.shape[1]
    half_width = model_width // lax.axis_size("pool")
    projection = gate_up[0].reshape(-1, model_width)
    hidden_size = projection.shape[0] // 2
    received = lax.all_to_all(
        outgoing_rows, ("req", "head"), split_axis=0, concat_axis=0, tiled=True
    )
    sources = received.shape[0]
    item_count = received.shape[1]
    flat_rows = received.reshape(sources * item_count, model_width)
    projected = jnp.einsum("nd,fd->nf", flat_rows, projection, preferred_element_type=jnp.float32)
    activated = (jax.nn.silu(projected[:, :hidden_size]) * projected[:, hidden_size:]).astype(
        jnp.bfloat16
    )
    part_sum = jnp.dot(activated, down_weight[0], preferred_element_type=jnp.float32).reshape(
        sources, item_count, model_width
    )
    column_sum = lax.psum_scatter(
        part_sum.astype(jnp.bfloat16), "pool", scatter_dimension=2, tiled=True
    )
    returned = lax.all_to_all(column_sum, ("req", "head"), split_axis=0, concat_axis=0, tiled=True)
    gathered = returned.reshape(expert_count * capacity, half_width).astype(jnp.float32)
    expert_mix = jnp.dot(combine_matrix, gathered, precision=lax.Precision.HIGHEST)
    own_columns = lax.dynamic_slice_in_dim(hidden, pool_index * half_width, half_width, 1)
    return (own_columns + expert_mix).astype(jnp.bfloat16)


def solution(mesh):
    return jax.shard_map(
        local,
        mesh=mesh,
        in_specs=(
            P(("group", "req"), "head"),
            P(("group", "req"), None, "head", None),
            P("head", ("group", "req", "pool"), None, None),
            P(("group", "req"), "pool", None),
            P(("group", "req"), "pool"),
            P(("group", "req", "pool")),
            P(("group", "req", "pool")),
            P(("group", "req", "head"), None),
            P(),
            P(("head", "pool"), None),
            P(("group", "req", "head"), None),
            P(("group", "req", "head"), None),
            P(("req", "head"), None, "pool", None),
            P(("req", "head"), "pool", None),
        ),
        out_specs=P(("group", "req", "head"), "pool"),
        check_vma=False,
    )
```

profile of v0, /device:TPU:0, one launch (start us, length us, event | category | flops | bytes accessed | tf_op | source)
XLA Modules:
  0.0 159.7 jit_solution(2999815218880634779)
XLA Ops:
  6.5 0.0 copy-start
  6.5 0.0 copy-start.2
  6.5 0.0 copy-start.4
  6.5 0.0 all-reduce.2.cloned.1.call-start
  6.5 1.2 copy.73
  7.7 0.7 compare_select_fusion.1
  8.4 0.5 gather_fusion
  8.9 0.6 collective-permute-start
  9.5 0.7 fusion.23
  10.2 0.7 compare_select_fusion.2
  10.8 0.7 iota_compare_fusion.2
  11.5 0.8 copy.59
  12.3 0.1 eq.33
  12.4 0.1 fusion.12
  12.5 0.1 reduce_window_sum.11
  12.6 0.2 select_reduce_fusion.1
  12.8 0.1 reduce_sum.59
  12.9 0.9 copy.64
  13.8 1.0 fusion.25
  14.8 0.0 copy-done.4
  14.8 0.1 copy.61
  14.9 0.0 collective-permute-done
  14.9 0.6 scatter_fusion
  15.5 0.6 gather_fusion.1
  16.1 0.3 fusion.24
  16.4 0.1 fusion.14
  16.5 0.0 copy-done.2
  16.6 0.2 fusion.15
  16.8 0.1 copy.54
  16.9 1.8 %all-gather.3 = bf16[2,48,8]{1,2,0:T(8,128)(2,1)S(1)} all-gather(bf16[1,48,8]{1,2,0:T(8,128)(2,1)S(1)} %copy.54), channel_id=3, replica_groups=mesh['group'=1,'req'=4,'head'=4,'pool'=2] {'pool'}, dimensions={0}, use_global_device_ids=true | all-gather | bytes 2304 | tf_op jit(solution)/shard_map/all_gather | solution.py:15
  18.7 0.2 fusion.7
  18.9 0.1 copy.57
  19.0 1.8 %all-gather.4 = bf16[2,48,8]{1,2,0:T(8,128)(2,1)S(1)} all-gather(bf16[1,48,8]{1,2,0:T(8,128)(2,1)S(1)} %copy.57), channel_id=4, replica_groups=mesh['group'=1,'req'=4,'head'=4,'pool'=2] {'pool'}, dimensions={0}, use_global_device_ids=true | all-gather | bytes 2304 | tf_op jit(solution)/shard_map/all_gather | solution.py:15
  20.9 0.1 copy.55
  21.0 0.1 copy.58
  21.0 0.1 copy.56
  21.1 0.3 fusion.2
  21.4 1.9 %all-gather = bf16[96,8,128]{2,1,0:T(8,128)(2,1)S(1)} all-gather(bf16[48,8,128]{2,1,0:T(8,128)(2,1)S(1)} %fusion.2), channel_id=2, replica_groups=mesh['group'=1,'req'=4,'head'=4,'pool'=2] {'pool'}, dimensions={0}, use_global_device_ids=true | all-gather | bytes 294912 | tf_op jit(solution)/shard_map/all_gather | solution.py:15
  23.3 0.0 copy-start.1
  23.3 0.2 divide_convert_fusion
  23.6 0.0 copy-start.3
  23.6 0.0 copy-done
  23.6 1.2 convolution_convert_fusion.2
  24.8 0.0 all-reduce.2.cloned.1.call-update
  24.8 0.0 reduce-scatter.2.cloned.1.call-start
  24.8 0.1 convert_reduce_fusion
  25.0 56.1 %all-reduce.2.cloned.1.call-done = bf16[48,2048]{1,0:T(8,128)(2,1)} async-done(((bf16[48,2048]{1,0:T(8,128)(2,1)}), bf16[48,2048]{1,0:T(8,128)(2,1)}) %all-reduce.2.cloned.1.call-update) | async-done | bytes 196624 | tf_op jit(solution)/shard_map/psum | solution.py:108
  81.0 0.0 copy-done.1
  81.0 1.0 multiply_reduce_fusion
  82.1 0.0 copy-done.3
  82.1 1.3 convolution_convert_fusion.1
  83.4 1.3 reshape.273
  84.6 30.5 %all_to_all.10 = bf16[16,12,2048]{2,1,0:T(8,128)(2,1)} all-to-all(bf16[16,12,2048]{2,1,0:T(8,128)(2,1)S(1)} %reshape.273), channel_id=1, replica_groups=mesh['group'=1,'req'=4,'head'=4,'pool'=2] {'req','head'}, dimensions={0} | all-to-all | bytes 1572864 | tf_op jit(solution)/shard_map/all_to_all | solution.py:138
  115.1 1.3 reshape.274
  116.4 2.1 %fusion.26 = f32[192,384]{1,0:T(8,128)S(1)} fusion(bf16[192,2048]{1,0:T(8,128)(2,1)S(1)} %reshape.274, bf16[384,2048]{1,0:T(8,128)(2,1)} %bitcast.85), kind=kOutput, calls=%fused_computation.71 | convolution fusion | flops 301989888 | bytes 2654208 | tf_op jit(solution)/shard_map/nd,fd->nf/dot_general | solution.py:144
  118.5 0.1 fusion.6
  118.7 2.4 %convolution_convert_fusion = bf16[16,12,2048]{2,0,1:T(8,128)(2,1)} fusion(bf16[1,192,2048]{2,1,0:T(8,128)(2,1)} %param.27, bf16[16,12,192]{2,1,0:T(8,128)(2,1)S(1)} %dot_general.36), kind=kOutput, calls=%fused_computation.3 | convolution fusion | flops 151388160 | bytes 1646592 | tf_op jit(solution)/shard_map/dot_general | solution.py:148
  121.0 0.0 reduce-scatter.2.cloned.1.call-update
  121.1 6.6 %reduce-scatter.2.cloned.1.call-done = bf16[16,12,1024]{2,0,1:T(8,128)(2,1)} async-done(((bf16[16,12,2048]{2,0,1:T(8,128)(2,1)}), bf16[16,12,1024]{2,0,1:T(8,128)(2,1)}) %reduce-scatter.2.cloned.1.call-update) | async-done | bytes 393232 | tf_op jit(solution)/shard_map/reduce_scatter | solution.py:151
  127.6 2.0 %copy.63 = bf16[16,12,1024]{2,1,0:T(8,128)(2,1)} copy(bf16[16,12,1024]{2,0,1:T(8,128)(2,1)} %reduce-scatter.2.cloned.1.call-done) | data formatting | bytes 786432 | tf_op jit(solution)/shard_map/reduce_scatter | solution.py:151
  129.6 6.7 %all-to-all-start.1 = ((bf16[16,12,1024]{2,1,0:T(8,128)(2,1)}), bf16[16,12,1024]{2,1,0:T(8,128)(2,1)S(1)}, u32[]{:S(2)}, u32[]{:S(2)}) async-start(bf16[16,12,1024]{2,1,0:T(8,128)(2,1)} %copy.63), calls=%async_computation.2 | async-start | bytes 1048576 | tf_op jit(solution)/shard_map/all_to_all | solution.py:154
  136.4 15.5 %all-to-all-done.1 = bf16[16,12,1024]{2,1,0:T(8,128)(2,1)S(1)} async-done(((bf16[16,12,1024]{2,1,0:T(8,128)(2,1)}), bf16[16,12,1024]{2,1,0:T(8,128)(2,1)S(1)}, u32[]{:S(2)}, u32[]{:S(2)}) %all-to-all-start.1) | async-done | bytes 393248 | tf_op jit(solution)/shard_map/all_to_all | solution.py:154
  151.9 0.1 reshape.275
  151.9 0.9 fusion.4
  (9 shorter events, 0.1 us)
Async XLA Ops:
  6.5 17.1 %copy-start = (bf16[512,2048]{1,0:T(8,128)(2,1)S(1)}, bf16[512,2048]{1,0:T(8,128)(2,1)}, u32[]{:S(2)}) copy-start(bf16[512,2048]{1,0:T(8,128)(2,1)} %param.23) | copy-start | bytes 6291460
  6.5 10.0 %copy-start.2 = (bf16[48,2,1,256]{3,1,2,0:T(2,128)(2,1)S(1)}, bf16[48,2,1,256]{3,1,2,0:T(2,128)(2,1)}, u32[]{:S(2)}) copy-start(bf16[48,2,1,256]{3,1,2,0:T(2,128)(2,1)} %param.15) | copy-start | bytes 147460
  6.5 8.3 %copy-start.4 = (f32[12,8]{0,1:T(8,128)S(1)}, f32[12,8]{0,1:T(8,128)}, u32[]{:S(2)}) copy-start(f32[12,8]{0,1:T(8,128)} %param.25) | copy-start | bytes 1156
  6.5 74.5 %all-reduce.2.cloned.1.call-start = ((), (), s32[]{:S(2)}) async-start(), calls=%async_computation.3 | async-start | bytes 393216 | tf_op jit(solution)/shard_map/psum | solution.py:108
  8.9 6.0 %collective-permute-start = (bf16[1,4,16,256]{3,2,1,0:T(8,128)(2,1)S(1)}, bf16[1,4,16,256]{3,2,1,0:T(8,128)(2,1)S(1)}, u32[]{:S(2)}, u32[]{:S(2)}) collective-permute-start(bf16[1,4,16,256]{3,2,1,0:T(8,128)(2,1)S(1)} %bitcast.94), channel_id=1, source_target_pairs={{0,1},{1,0},{2,3},{3,2},{4,5},{5,4},{6,7},{7,6},{8,9},{9,8},{10,11... | collective-permute-start | bytes 98312 | tf_op jit(solution)/shard_map/ppermute | solution.py:10
  23.3 57.7 %copy-start.1 = (bf16[12,2048]{1,0:T(8,128)(2,1)S(1)}, bf16[12,2048]{1,0:T(8,128)(2,1)}, u32[]{:S(2)}) copy-start(bf16[12,2048]{1,0:T(8,128)(2,1)} %param.21) | copy-start | bytes 147460
  23.6 58.5 %copy-start.3 = (f32[2048]{0:T(1024)S(1)}, f32[2048]{0:T(1024)}, u32[]{:S(2)}) copy-start(f32[2048]{0:T(1024)} %param.22) | copy-start | bytes 24580
  24.8 102.8 %reduce-scatter.2.cloned.1.call-start = ((), (), s32[]{:S(2)}) async-start(), calls=%async_computation.4 | async-start | bytes 1179648 | tf_op jit(solution)/shard_map/reduce_scatter | solution.py:151
  129.6 22.2 %all-to-all-start.1 = ((bf16[16,12,1024]{2,1,0:T(8,128)(2,1)}), bf16[16,12,1024]{2,1,0:T(8,128)(2,1)S(1)}, u32[]{:S(2)}, u32[]{:S(2)}) async-start(bf16[16,12,1024]{2,1,0:T(8,128)(2,1)} %copy.63), calls=%async_computation.2 | async-start | bytes 1048576 | tf_op jit(solution)/shard_map/all_to_all | solution.py:154
Sparse Core Ops, SparseCore 0:
  24.9 56.0 all-reduce.1
  121.2 6.3 reduce-scatter.1
where the time goes:
time: 160 us
  waiting for transfers between devices  78.1 us (49%)
  blocking collectives  36.1 us (23%)
  between operations  13.6 us (8%)
  local copies, waits for them, and re-layouts  10 us (6%)
  matrix products  9.56 us (6%)
  starting transfers between devices  7.33 us (5%)
  other arithmetic  4.95 us (3%)
    psum x1, waiting for transfers between devices, local(): lax.psum(partial_value.astype(jnp.bfloat16), ('head', 'pool'))  56.1 us
    all_to_all x1, blocking collectives, local(): lax.all_to_all(outgoing_rows, ('req', 'head'), split_axis=0, concat_axis=...  30.5 us
    all_to_all x1, waiting for transfers between devices, local(): lax.all_to_all(column_sum, ('req', 'head'), split_axis=0, concat_axis=0,...  15.5 us
    all_to_all x1, starting transfers between devices, local(): lax.all_to_all(column_sum, ('req', 'head'), split_axis=0, concat_axis=0,...  6.73 us
    reduce_scatter x1, waiting for transfers between devices, local(): lax.psum_scatter(part_sum.astype(jnp.bfloat16), 'pool', scatter_dimension...  6.55 us
    all_gather x3, blocking collectives, combined_all(): lax.all_gather(a.astype(kind), axis)  5.63 us
  transfers between devices with their start and end apart: 4, of which 3 were waited for; matrix products, arithmetic and copies ran while one was open for 3% of the time, Pallas kernels for 0%

commit v1 on v0

--- a/solution.py
+++ b/solution.py
@@ -105,7 +105,9 @@
     own_heads = lax.dynamic_slice_in_dim(attended, pool_index * head_width, head_width, 1)
     partial_value = jnp.dot(own_heads, output_weight, preferred_element_type=jnp.float32)
     rows_here = residual.shape[0]
-    summed = lax.psum(partial_value.astype(jnp.bfloat16), ("head", "pool")).astype(jnp.float32)
+    summed = lax.psum(lax.psum(partial_value.astype(jnp.bfloat16), "pool"), "head").astype(
+        jnp.float32
+    )
     attention = lax.dynamic_slice_in_dim(summed, lax.axis_index("head") * rows_here, rows_here, 0)
     hidden = residual.astype(jnp.float32) + attention
     normed = (

time: 160 us -> 172 us (1.075)
  waiting for transfers between devices: 78.1 us -> 88.7 us
    psum x1 -> x2, waiting for transfers between devices: 56.1 us -> 66.5 us  [the longest x1 46.4 us: local(): lax.psum(lax.psum(partial_value.astype(jnp.bfloat16), 'pool'), 'head')]
  transfers between devices with their start and end apart: 4 -> 5, of which waited for: 3 -> 4; matrix products, arithmetic and copies ran while one was open for 3% -> 3% of each run, Pallas kernels for 0% -> 0%
where the time goes in v1:
time: 172 us; the launch traced here: 171 us
  waiting for transfers between devices  88.7 us (52%)
  blocking collectives  37 us (22%)
  between operations  13.4 us (8%)
  local copies, waits for them, and re-layouts  10 us (6%)
  matrix products  9.57 us (6%)
  starting transfers between devices  7.38 us (4%)
  other arithmetic  4.94 us (3%)
    psum x1, waiting for transfers between devices, local(): lax.psum(lax.psum(partial_value.astype(jnp.bfloat16), 'pool'), 'head')  46.4 us
    all_to_all x1, blocking collectives, local(): lax.all_to_all(outgoing_rows, ('req', 'head'), split_axis=0, concat_axis=...  31.3 us
    psum x1, waiting for transfers between devices, local(): lax.psum(partial_value.astype(jnp.bfloat16), 'pool')  20.1 us
    all_to_all x1, waiting for transfers between devices, local(): lax.all_to_all(column_sum, ('req', 'head'), split_axis=0, concat_axis=0,...  15.5 us
    all_to_all x1, starting transfers between devices, local(): lax.all_to_all(column_sum, ('req', 'head'), split_axis=0, concat_axis=0,...  6.74 us
    reduce_scatter x1, waiting for transfers between devices, local(): lax.psum_scatter(part_sum.astype(jnp.bfloat16), 'pool', scatter_dimension...  6.66 us
    all_gather x3, blocking collectives, combined_all(): lax.all_gather(a.astype(kind), axis)  5.63 us
  transfers between devices with their start and end apart: 5, of which 4 were waited for; matrix products, arithmetic and copies ran while one was open for 3% of the time, Pallas kernels for 0%

profile of v1, /device:TPU:0, one launch (start us, length us, event | category | flops | bytes accessed | tf_op | source)
XLA Modules:
  0.0 170.9 jit_solution(14365725323530638952)
XLA Ops:
  6.5 0.0 copy-start
  6.5 0.0 all-reduce.3.cloned.1.call-start
  6.5 1.2 copy.74
  7.7 0.7 compare_select_fusion.1
  8.4 0.5 gather_fusion
  8.9 0.6 collective-permute-start
  9.5 0.7 fusion.23
  10.2 0.7 compare_select_fusion.2
  10.8 0.7 iota_compare_fusion.2
  11.5 0.9 copy.64
  12.5 1.0 fusion.25
  13.4 0.8 copy.59
  14.2 0.1 eq.33
  14.3 0.0 collective-permute-done
  14.3 0.6 scatter_fusion
  14.9 0.6 gather_fusion.1
  15.5 0.3 fusion.24
  15.8 0.1 fusion.14
  15.9 0.0 copy-done.2
  15.9 0.2 fusion.15
  16.2 0.1 copy.54
  16.3 1.8 %all-gather.3 = bf16[2,48,8]{1,2,0:T(8,128)(2,1)S(1)} all-gather(bf16[1,48,8]{1,2,0:T(8,128)(2,1)S(1)} %copy.54), channel_id=3, replica_groups=mesh['group'=1,'req'=4,'head'=4,'pool'=2] {'pool'}, dimensions={0}, use_global_device_ids=true | all-gather | bytes 2304 | tf_op jit(solution)/shard_map/all_gather | solution.py:15
  18.1 0.2 fusion.7
  18.3 0.1 copy.57
  18.4 1.8 %all-gather.4 = bf16[2,48,8]{1,2,0:T(8,128)(2,1)S(1)} all-gather(bf16[1,48,8]{1,2,0:T(8,128)(2,1)S(1)} %copy.57), channel_id=4, replica_groups=mesh['group'=1,'req'=4,'head'=4,'pool'=2] {'pool'}, dimensions={0}, use_global_device_ids=true | all-gather | bytes 2304 | tf_op jit(solution)/shard_map/all_gather | solution.py:15
  20.3 0.1 copy.55
  20.3 0.1 copy.58
  20.4 0.1 copy.56
  20.5 0.3 fusion.2
  20.8 1.9 %all-gather = bf16[96,8,128]{2,1,0:T(8,128)(2,1)S(1)} all-gather(bf16[48,8,128]{2,1,0:T(8,128)(2,1)S(1)} %fusion.2), channel_id=2, replica_groups=mesh['group'=1,'req'=4,'head'=4,'pool'=2] {'pool'}, dimensions={0}, use_global_device_ids=true | all-gather | bytes 294912 | tf_op jit(solution)/shard_map/all_gather | solution.py:15
  22.7 0.2 divide_convert_fusion
  22.9 0.0 copy-start.4
  23.0 0.0 copy-start.1
  23.0 0.0 copy-done
  23.0 0.0 copy-start.3
  23.0 1.2 convolution_convert_fusion.2
  24.2 0.0 all-reduce.3.cloned.1.call-update
  24.2 0.0 all-reduce.5.cloned.1.call-start
  24.3 0.1 fusion.12
  24.3 0.1 reduce_window_sum.11
  24.5 0.2 select_reduce_fusion.1
  24.7 0.1 reduce_sum.59
  24.7 20.1 %all-reduce.3.cloned.1.call-done = bf16[48,2048]{1,0:T(8,128)(2,1)} async-done(((bf16[48,2048]{1,0:T(8,128)(2,1)}), bf16[48,2048]{1,0:T(8,128)(2,1)}) %all-reduce.3.cloned.1.call-update) | async-done | bytes 196624 | tf_op jit(solution)/shard_map/psum | solution.py:108
  44.8 0.0 all-reduce.5.cloned.1.call-update
  44.9 0.0 reduce-scatter.2.cloned.1.call-start
  44.9 0.0 copy-done.4
  44.9 0.1 copy.61
  45.0 0.1 convert_reduce_fusion
  45.1 46.4 %all-reduce.5.cloned.1.call-done = bf16[48,2048]{1,0:T(8,128)(2,1)} async-done(((bf16[48,2048]{1,0:T(8,128)(2,1)}), bf16[48,2048]{1,0:T(8,128)(2,1)}) %all-reduce.5.cloned.1.call-update) | async-done | bytes 196624 | tf_op jit(solution)/shard_map/psum | solution.py:108
  91.5 1.0 multiply_reduce_fusion
  92.6 1.3 convolution_convert_fusion.1
  93.9 1.3 reshape.273
  95.2 31.3 %all_to_all.10 = bf16[16,12,2048]{2,1,0:T(8,128)(2,1)} all-to-all(bf16[16,12,2048]{2,1,0:T(8,128)(2,1)S(1)} %reshape.273), channel_id=1, replica_groups=mesh['group'=1,'req'=4,'head'=4,'pool'=2] {'req','head'}, dimensions={0} | all-to-all | bytes 1572864 | tf_op jit(solution)/shard_map/all_to_all | solution.py:140
  126.5 1.3 reshape.274
  127.8 2.1 %fusion.26 = f32[192,384]{1,0:T(8,128)S(1)} fusion(bf16[192,2048]{1,0:T(8,128)(2,1)S(1)} %reshape.274, bf16[384,2048]{1,0:T(8,128)(2,1)} %bitcast.85), kind=kOutput, calls=%fused_computation.71 | convolution fusion | flops 301989888 | bytes 2654208 | tf_op jit(solution)/shard_map/nd,fd->nf/dot_general | solution.py:146
  129.9 0.1 fusion.6
  130.1 2.4 %convolution_convert_fusion = bf16[16,12,2048]{2,0,1:T(8,128)(2,1)} fusion(bf16[1,192,2048]{2,1,0:T(8,128)(2,1)} %param.27, bf16[16,12,192]{2,1,0:T(8,128)(2,1)S(1)} %dot_general.36), kind=kOutput, calls=%fused_computation.3 | convolution fusion | flops 151388160 | bytes 1646592 | tf_op jit(solution)/shard_map/dot_general | solution.py:150
  132.5 0.0 reduce-scatter.2.cloned.1.call-update
  132.5 6.7 %reduce-scatter.2.cloned.1.call-done = bf16[16,12,1024]{2,0,1:T(8,128)(2,1)} async-done(((bf16[16,12,2048]{2,0,1:T(8,128)(2,1)}), bf16[16,12,1024]{2,0,1:T(8,128)(2,1)}) %reduce-scatter.2.cloned.1.call-update) | async-done | bytes 393232 | tf_op jit(solution)/shard_map/reduce_scatter | solution.py:153
  139.1 2.0 %copy.63 = bf16[16,12,1024]{2,1,0:T(8,128)(2,1)} copy(bf16[16,12,1024]{2,0,1:T(8,128)(2,1)} %reduce-scatter.2.cloned.1.call-done) | data formatting | bytes 786432 | tf_op jit(solution)/shard_map/reduce_scatter | solution.py:153
  141.2 6.7 %all-to-all-start.1 = ((bf16[16,12,1024]{2,1,0:T(8,128)(2,1)}), bf16[16,12,1024]{2,1,0:T(8,128)(2,1)S(1)}, u32[]{:S(2)}, u32[]{:S(2)}) async-start(bf16[16,12,1024]{2,1,0:T(8,128)(2,1)} %copy.63), calls=%async_computation.2 | async-start | bytes 1048576 | tf_op jit(solution)/shard_map/all_to_all | solution.py:156
  147.9 15.5 %all-to-all-done.1 = bf16[16,12,1024]{2,1,0:T(8,128)(2,1)S(1)} async-done(((bf16[16,12,1024]{2,1,0:T(8,128)(2,1)}), bf16[16,12,1024]{2,1,0:T(8,128)(2,1)S(1)}, u32[]{:S(2)}, u32[]{:S(2)}) %all-to-all-start.1) | async-done | bytes 393248 | tf_op jit(solution)/shard_map/all_to_all | solution.py:156
  163.4 0.1 reshape.275
  163.5 0.9 fusion.4
  (12 shorter events, 0.1 us)
Async XLA Ops:
  6.5 16.5 %copy-start = (bf16[512,2048]{1,0:T(8,128)(2,1)S(1)}, bf16[512,2048]{1,0:T(8,128)(2,1)}, u32[]{:S(2)}) copy-start(bf16[512,2048]{1,0:T(8,128)(2,1)} %param.23) | copy-start | bytes 6291460
  6.5 9.4 %copy-start.2 = (bf16[48,2,1,256]{3,1,2,0:T(2,128)(2,1)S(1)}, bf16[48,2,1,256]{3,1,2,0:T(2,128)(2,1)}, u32[]{:S(2)}) copy-start(bf16[48,2,1,256]{3,1,2,0:T(2,128)(2,1)} %param.15) | copy-start | bytes 147460
  6.5 38.3 %all-reduce.3.cloned.1.call-start = ((), (), s32[]{:S(2)}) async-start(), calls=%async_computation.3 | async-start | bytes 393216 | tf_op jit(solution)/shard_map/psum | solution.py:108
  8.9 5.4 %collective-permute-start = (bf16[1,4,16,256]{3,2,1,0:T(8,128)(2,1)S(1)}, bf16[1,4,16,256]{3,2,1,0:T(8,128)(2,1)S(1)}, u32[]{:S(2)}, u32[]{:S(2)}) collective-permute-start(bf16[1,4,16,256]{3,2,1,0:T(8,128)(2,1)S(1)} %bitcast.94), channel_id=1, source_target_pairs={{0,1},{1,0},{2,3},{3,2},{4,5},{5,4},{6,7},{7,6},{8,9},{9,8},{10,11... | collective-permute-start | bytes 98312 | tf_op jit(solution)/shard_map/ppermute | solution.py:10
  22.9 22.0 %copy-start.4 = (f32[12,8]{0,1:T(8,128)S(1)}, f32[12,8]{0,1:T(8,128)}, u32[]{:S(2)}) copy-start(f32[12,8]{0,1:T(8,128)} %param.25) | copy-start | bytes 1156
  23.0 68.6 %copy-start.1 = (bf16[12,2048]{1,0:T(8,128)(2,1)S(1)}, bf16[12,2048]{1,0:T(8,128)(2,1)}, u32[]{:S(2)}) copy-start(bf16[12,2048]{1,0:T(8,128)(2,1)} %param.21) | copy-start | bytes 147460
  23.0 69.6 %copy-start.3 = (f32[2048]{0:T(1024)S(1)}, f32[2048]{0:T(1024)}, u32[]{:S(2)}) copy-start(f32[2048]{0:T(1024)} %param.22) | copy-start | bytes 24580
  24.2 67.3 %all-reduce.5.cloned.1.call-start = ((), (), s32[]{:S(2)}) async-start(), calls=%async_computation.4 | async-start | bytes 393216 | tf_op jit(solution)/shard_map/psum | solution.py:108
  44.9 94.3 %reduce-scatter.2.cloned.1.call-start = ((), (), s32[]{:S(2)}) async-start(), calls=%async_computation.5 | async-start | bytes 1179648 | tf_op jit(solution)/shard_map/reduce_scatter | solution.py:153
  141.2 22.2 %all-to-all-start.1 = ((bf16[16,12,1024]{2,1,0:T(8,128)(2,1)}), bf16[16,12,1024]{2,1,0:T(8,128)(2,1)S(1)}, u32[]{:S(2)}, u32[]{:S(2)}) async-start(bf16[16,12,1024]{2,1,0:T(8,128)(2,1)} %copy.63), calls=%async_computation.2 | async-start | bytes 1048576 | tf_op jit(solution)/shard_map/all_to_all | solution.py:156
Sparse Core Ops, SparseCore 0:
  24.3 20.4 all-reduce.2
  47.7 43.7 all-reduce.4
  132.6 6.4 reduce-scatter.1
